TPU v7x, 512 devices: a whole 4x4x16 slice. The times are simulated.
512 devices in a mesh: dp: 64 (over x, z), expert: 8 (over y, core).
Axes of the slice: x: 4, y: 4, z: 16, core: 2. Of those that a mesh axis runs over, the one named last changes fastest.
Arguments:
- grad_out: bfloat16 [131072, 1024], P(('dp', 'expert')), may hold values from -1 to 1
- routes: int32 [131072, 6], P(('dp', 'expert')), may hold values from 0 to 63, all different within a row; in each aligned block of 256 rows (0 to 255, 256 to 511, ...) at most 48 rows name the same one
- route_weight: float32 [131072, 6], P(('dp', 'expert')), may hold values from 0.05 to 0.35
- example_ids: int32 [64, 2048], P('dp', 'expert'), may hold values from 0 to 7, never falling along the last dimension, each value on 1 to 512 neighbouring positions
- example_weight: float32 [64, 8], P('dp'), may hold values from 0.5 to 50
- hidden: bfloat16 [64, 8, 8, 48, 704], P('dp', 'expert'), may hold values from -6 to 6
Outputs:
- expert_grads: float32 [704, 8, 1024], P('dp', 'expert')
Inputs may be any that keep to these rules, and one draw needn't show every extreme that they name: `routes`: each row names 6 different experts; in the rows of one device no expert is named more than 48 times, a bound that some block reaches. `example_ids`: along a data group's tokens the numbers never fall; each of the 8 examples has from 1 to a quarter of 2048 tokens, one exactly that many.
All inputs are finite; a program needn't handle non-finite values.
Results may differ from a plain program's by a relative error of at most 0.0011.
Values may be sent and summed in bfloat16 or wider, within the bound.
A program may use at most 64 MiB of HBM per device.

v0:
```python
import jax
import jax.numpy as jnp
from jax import lax
from jax.sharding import PartitionSpec as P

FF_WIN = 704
D_WIN = 1024
EXAMPLES = 8


def slot_layout(block_routes, expert_list, capacity):
    matches = (block_routes[..., None] == expert_list).astype(jnp.float32)
    routed = jnp.sum(matches, axis=-2)
    ranking = jnp.cumsum(routed, axis=-2) - routed
    slot_index = jnp.arange(capacity).astype(jnp.float32)
    placed = routed[..., None] * (ranking[..., None] == slot_index).astype(jnp.float32)
    return (matches, placed)


def shards(grad_out, routes, route_weight, example_ids, example_weight, hidden):
    highest = lax.Precision.HIGHEST
    sources = lax.axis_size("expert")
    device = lax.axis_index("expert")
    tokens_here = grad_out.shape[0]
    top_count = routes.shape[1]
    local_experts = hidden.shape[1]
    capacity = hidden.shape[3]
    slot_total = sources * capacity
    in_flight = jnp.arange(sources * local_experts, dtype=jnp.int32)
    example_index = jnp.arange(EXAMPLES, dtype=jnp.int32)
    own_ids = example_ids.reshape(tokens_here)
    own_members = (own_ids[:, None] == example_index).astype(jnp.float32)
    token_weight = jnp.sum(own_members * example_weight[0], axis=1)
    matches, placed = slot_layout(routes, in_flight, capacity)
    token_scale = jnp.sum(matches * route_weight[:, :, None], axis=1) * token_weight[:, None]
    dispatch = placed.astype(jnp.bfloat16)
    slot_rows = jnp.einsum("tec,td->ecd", dispatch, grad_out, preferred_element_type=jnp.float32)
    slot_scale = jnp.sum(placed * token_scale[:, :, None], axis=0)
    outgoing = (
        (slot_rows * slot_scale[:, :, None])
        .astype(jnp.bfloat16)
        .reshape(sources, local_experts, capacity, D_WIN)
    )
    incoming = lax.all_to_all(outgoing, "expert", split_axis=0, concat_axis=0, tiled=True)
    group_routes, group_ids = (
        lax.all_gather(routes, "expert", axis=0, tiled=True),
        lax.all_gather(own_ids, "expert", axis=0, tiled=True),
    )
    own_experts = device * local_experts + jnp.arange(local_experts, dtype=jnp.int32)
    unused_matches, group_placed = slot_layout(
        group_routes.reshape(sources, tokens_here, top_count), own_experts, capacity
    )
    group_members = (group_ids.reshape(sources, tokens_here)[:, :, None] == example_index).astype(
        jnp.float32
    )
    member = jnp.einsum("stjc,stx->jscx", group_placed, group_members, precision=highest).reshape(
        local_experts, slot_total, EXAMPLES
    )
    acts_slots = hidden[0].reshape(local_experts, slot_total, FF_WIN)
    cot_slots = jnp.transpose(incoming, (1, 0, 2, 3)).reshape(local_experts, slot_total, D_WIN)
    pieces = []
    for example in range(EXAMPLES):
        chosen = jnp.where(
            member[:, :, example : example + 1] > 0.5, cot_slots, jnp.zeros_like(cot_slots)
        )
        own_grad = jnp.einsum(
            "jif,jid->jfd", acts_slots, chosen, preferred_element_type=jnp.float32
        )
        pieces.append(jnp.sum(own_grad * own_grad))
    squares = jnp.stack(pieces)
    total_squares = lax.psum(squares, "expert")
    clip_factor = 1.0 / jnp.maximum(jnp.sqrt(total_squares / (FF_WIN * D_WIN)), 1.0)
    slot_weight = jnp.sum(member * clip_factor, axis=2) / EXAMPLES
    scaled = (slot_weight[:, :, None] * cot_slots.astype(jnp.float32)).astype(jnp.bfloat16)
    return lax.psum_scatter(
        jnp.einsum("jif,jid->fjd", acts_slots, scaled, preferred_element_type=jnp.float32),
        "dp",
        scatter_dimension=0,
        tiled=True,
    )


def solution(mesh):
    placed = (
        P(("dp", "expert"), None),
        P(("dp", "expert"), None),
        P(("dp", "expert"), None),
        P("dp", "expert"),
        P("dp", None),
        P("dp", "expert", None, None, None),
    )
    return jax.shard_map(
        shards, mesh=mesh, in_specs=placed, out_specs=P("dp", "expert", None), check_vma=False
    )
```

profile of v0, /device:TPU:24, one launch (start us, length us, event | category | flops | bytes accessed | tf_op | source)
XLA Modules:
  0.0 382.1 jit_solution(6977054761637822390)
XLA Ops:
  6.5 0.8 convert_reduce_fusion.1
  7.3 0.6 reduce-window.16
  8.1 0.8 select_reduce_fusion.1
  9.2 2.3 fusion
  11.5 9.0 %all-to-all-start = ((bf16[8,1,48,1024]{3,2,1,0:T(8,128)(2,1)}), bf16[8,1,48,1024]{3,2,1,0:T(8,128)(2,1)S(1)}, u32[]{:S(2)}, u32[]{:S(2)}) async-start(bf16[8,1,48,1024]{3,2,1,0:T(8,128)(2,1)} %fusion), calls=%async_computation | async-start | bytes 1572864 | tf_op jit(solution)/shard_map/all_to_all | solution.py:44
  20.6 17.8 %all_gather.7 = s32[2048,6]{0,1:T(8,128)S(1)} all-gather(s32[256,6]{0,1:T(8,128)S(1)} %copy-done.1), channel_id=1, replica_groups=mesh['dp'=64,'expert'=8] {'expert'}, dimensions={0}, use_global_device_ids=true | all-gather | bytes 55296 | tf_op jit(solution)/shard_map/all_gather | solution.py:46
  38.4 0.6 reduce-window.14
  39.2 7.8 %all-gather = s32[1,2048]{1,0:T(1,128)S(1)} all-gather(s32[1,256]{1,0:T(1,128)S(1)} %copy-done.2), channel_id=2, replica_groups=mesh['dp'=64,'expert'=8] {'expert'}, dimensions={1}, use_global_device_ids=true | all-gather | bytes 9216 | tf_op jit(solution)/shard_map/all_gather | solution.py:47
  47.5 0.7 reduce.50
  48.8 2.0 multiply_reduce_fusion
  50.8 2.0 multiply_reduce_fusion.1
  52.8 2.0 multiply_reduce_fusion.2
  54.8 2.0 multiply_reduce_fusion.3
  56.8 2.0 multiply_reduce_fusion.4
  58.8 2.0 multiply_reduce_fusion.5
  60.8 2.0 multiply_reduce_fusion.6
  62.8 2.0 multiply_reduce_fusion.7
  64.8 5.0 %stack.35 = f32[8]{0:T(128)S(1)} concatenate(f32[1]{0:T(128)} %bitcast.19, f32[1]{0:T(128)} %bitcast.21, f32[1]{0:T(128)} %bitcast.23, f32[1]{0:T(128)} %bitcast.25, f32[1]{0:T(128)} %bitcast.27, f32[1]{0:T(128)} %bitcast.29, f32[1]{0:T(128)} %bitcast.31, f32[1]{0:T(128)} %bitcast.33), dimensions={0} | concatenate | bytes 64 | tf_op jit(solution)/shard_map/stack | solution.py:70
  69.8 11.9 %psum.7 = f32[8]{0:T(128)S(1)} all-reduce(f32[8]{0:T(128)S(1)} %stack.35), channel_id=1, replica_groups=mesh['dp'=64,'expert'=8] {'expert'}, use_global_device_ids=true, to_apply=%region_17.18 | all-reduce | flops 8 | bytes 64 | tf_op jit(solution)/shard_map/psum | solution.py:71
  81.9 1.0 convolution_bitcast_fusion
  82.9 4.6 %copy.24 = f32[704,1,1024]{2,1,0:T(1,128)} copy(f32[704,1,1024]{2,0,1:T(8,128)S(1)} %convolution_bitcast_fusion) | data formatting | bytes 5767168 | tf_op jit(solution)/shard_map/jif,jid->fjd/transpose | solution.py:76
  87.5 1.3 dynamic-slice
  89.5 284.4 %all-reduce.3.cloned.1.call-done = f32[704,1,1024]{2,1,0:T(1,128)} async-done(((f32[704,1,1024]{2,1,0:T(1,128)}), f32[704,1,1024]{2,1,0:T(1,128)}) %all-reduce.3.cloned.1.call-update) | async-done | bytes 2883600
  373.9 1.4 constant_dynamic-slice_fusion
  (32 shorter events, 2.0 us)
Async XLA Ops:
  6.5 42.3 %copy-start = (bf16[1,1,8,48,704]{4,3,2,1,0:T(8,128)(2,1)S(1)}, bf16[1,1,8,48,704]{4,3,2,1,0:T(8,128)(2,1)}, u32[]{:S(2)}) copy-start(bf16[1,1,8,48,704]{4,3,2,1,0:T(8,128)(2,1)} %param.11) | copy-start | bytes 1622020
  6.5 14.0 %copy-start.1 = (s32[256,6]{0,1:T(8,128)S(1)}, s32[256,6]{0,1:T(8,128)}, u32[]{:S(2)}) copy-start(s32[256,6]{0,1:T(8,128)} %param.7) | copy-start | bytes 18436
  6.5 32.6 %copy-start.2 = (s32[1,256]{1,0:T(1,128)S(1)}, s32[1,256]{1,0:T(1,128)}, u32[]{:S(2)}) copy-start(s32[1,256]{1,0:T(1,128)} %param.9) | copy-start | bytes 3076
  11.5 37.3 %all-to-all-start = ((bf16[8,1,48,1024]{3,2,1,0:T(8,128)(2,1)}), bf16[8,1,48,1024]{3,2,1,0:T(8,128)(2,1)S(1)}, u32[]{:S(2)}, u32[]{:S(2)}) async-start(bf16[8,1,48,1024]{3,2,1,0:T(8,128)(2,1)} %fusion), calls=%async_computation | async-start | bytes 1572864 | tf_op jit(solution)/shard_map/all_to_all | solution.py:44
  20.6 353.3 %all-reduce.3.cloned.1.call-start = ((), (), s32[]{:S(2)}) async-start(), calls=%async_computation.1 | async-start | bytes 5767168
Sparse Core Ops, SparseCore 0:
  87.6 286.1 all-reduce.2
where the time goes:
time: 383 us; the launch traced here: 382 us
  waiting for transfers between devices  284 us (74%)
  blocking collectives  37.5 us (10%)
  matrix products  19.7 us (5%)
  between operations  14.2 us (4%)
  local copies, waits for them, and re-layouts  13.3 us (3%)
  starting transfers between devices  9.05 us (2%)
  other arithmetic  4.01 us (1%)
    unnamed x2, waiting for transfers between devices  284 us
    all_gather x1, blocking collectives, shards(): lax.all_gather(routes, 'expert', axis=0, tiled=True)  17.8 us
    dot_general x8, matrix products, shards(): jnp.einsum('jif,jid->jfd', acts_slots, chosen, preferred_element_type=jnp...  15.9 us
    psum x1, blocking collectives, shards(): total_squares = lax.psum(squares, 'expert')  11.9 us
    all_to_all x1, starting transfers between devices, shards(): lax.all_to_all(outgoing, 'expert', split_axis=0, concat_axis=0, tiled=True)  9.05 us
    all_gather x1, blocking collectives, shards(): lax.all_gather(own_ids, 'expert', axis=0, tiled=True)  7.79 us
  transfers between devices with their start and end apart: 2, of which 1 were waited for; matrix products, arithmetic and copies ran while one was open for 1% of the time, Pallas kernels for 0%

commit v1 on v0

v1 whole, which is shorter than its diff:
```python
import functools

import jax
import jax.numpy as jnp
from jax import lax
from jax.experimental import pallas as pl
from jax.experimental.pallas import tpu as pltpu
from jax.sharding import PartitionSpec as P

EXAMPLES = 8
TOP = 6
NX = 4
MESH = pl.DeviceIdType.MESH
F32 = jnp.float32
BF16 = jnp.bfloat16

REL = ((2, 0), (2, 1), (1, 0), (3, 0), (1, 1), (3, 1), (0, 1), (0, 0))


def nt_dot(a, b):
    return lax.dot_general(a, b, (((1,), (1,)), ((), ())), preferred_element_type=F32)


def nn_dot(a, b):
    return lax.dot_general(a, b, (((1,), (0,)), ((), ())), preferred_element_type=F32)


def iota(shape, dim):
    return lax.broadcasted_iota(jnp.int32, shape, dim)


def other(src, dst, send_sem, recv_sem, **device):
    return pltpu.make_async_remote_copy(
        src_ref=src, dst_ref=dst, send_sem=send_sem, recv_sem=recv_sem,
        device_id=device, device_id_type=MESH,
    )


def body(
    cfg,
    go_ref, routes_ref, weight_ref, ids_ref, ew_ref, h_ref,
    out_ref,
    h_buf, rank_s, scale_s, lo_s, hi_s, send_buf, c_buf, meta_send, meta_recv, sq_send, sq_recv,
    gl_s, ht_s, scaled_s,
    acc_a, ax_opp, ax_dir, azp, azm,
    h_sem, c_send, c_recv, m_send, m_recv, q_send, q_recv,
    ax_send, ax_recv, azp_send, azp_recv, azm_send, azm_recv,
):
    nz, ff, dw, cap, tok = cfg
    half_ring = nz // 2
    dp, me = lax.axis_index("dp"), lax.axis_index("expert")
    x, z = dp // nz, dp % nz
    y, core = me // 2, me % 2
    xp, xm, x2 = (x + 1) % NX, (x + 3) % NX, (x + 2) % NX
    zp, zm = (z + 1) % nz, (z + nz - 1) % nz
    at_xp, at_xm = dict(dp=xp * nz + z), dict(dp=xm * nz + z)
    at_zp, at_zm = dict(dp=x * nz + zp), dict(dp=x * nz + zm)
    dest = [((y + dy) % 4) * 2 + (core + dc) % 2 for dy, dc in REL]
    source = [((y + 4 - dy) % 4) * 2 + (core + 2 - dc) % 2 for dy, dc in REL]

    barrier = pltpu.get_barrier_semaphore()
    for p in range(7):
        pl.semaphore_signal(barrier, inc=1, device_id={"expert": dest[p]}, device_id_type=MESH)
    for place in (at_xp, at_xm, at_zp, at_zm):
        pl.semaphore_signal(barrier, inc=1, device_id=place, device_id_type=MESH)

    h_copies = [
        pltpu.make_async_copy(h_ref.at[source[p]], h_buf.at[p], h_sem.at[p]) for p in range(8)
    ]
    for copy in h_copies:
        copy.start()

    expert_row = iota((8, tok), 0)
    routed = jnp.zeros((8, tok), F32)
    weight = jnp.zeros((8, tok), F32)
    for k in range(TOP):
        match = routes_ref[k : k + 1, :] == expert_row
        routed = jnp.where(match, 1.0, routed)
        weight = jnp.where(match, weight_ref[k : k + 1, :], weight)
    ids = ids_ref[...]
    token_weight = jnp.zeros((1, tok), F32)
    for example in range(EXAMPLES):
        token_weight = jnp.where(
            ids == example, ew_ref[0:1, example : example + 1], token_weight
        )
    earlier = (iota((tok, tok), 0) < iota((tok, tok), 1)).astype(F32).astype(BF16)
    routed_b = routed.astype(BF16)
    rank = nn_dot(routed_b, earlier)
    rank_s[...] = jnp.where(routed > 0.5, rank, -1.0)
    scale_s[...] = weight * token_weight
    example_col = iota((128, tok), 0)
    lo_s[...] = nt_dot(routed_b, (ids < example_col).astype(F32).astype(BF16))
    hi_s[...] = nt_dot(routed_b, (ids <= example_col).astype(F32).astype(BF16))

    slot_col = iota((cap, tok), 0).astype(F32)
    sub8 = iota((8, 128), 0)
    c_copies, m_copies = [], []
    for p in range(7):
        c_copies.append(
            other(send_buf.at[p], c_buf.at[p], c_send.at[p], c_recv.at[p], expert=dest[p])
        )
        m_copies.append(
            other(meta_send.at[p], meta_recv.at[p], m_send.at[p], m_recv.at[p], expert=dest[p])
        )
    for batch in ((0, 1, 2, 3), (4, 5, 6, 7)):
        masks, scales = [], []
        for p in batch:
            hit = rank_s[pl.ds(dest[p], 1), :] == slot_col
            masks.append(hit.astype(F32).astype(BF16))
            scales.append(
                jnp.sum(jnp.where(hit, scale_s[pl.ds(dest[p], 1), :], 0.0), axis=1, keepdims=True)
            )
        rows = nn_dot(jnp.concatenate(masks, axis=0), go_ref[...])
        if batch[0] == 0:
            pl.semaphore_wait(barrier, 11)
        for i, p in enumerate(batch):
            value = (rows[i * cap : (i + 1) * cap, :] * scales[i]).astype(BF16)
            bounds = jnp.where(
                sub8 == 0, lo_s[pl.ds(dest[p], 1), :], hi_s[pl.ds(dest[p], 1), :]
            )
            if p == 7:
                c_buf[7] = value
                meta_recv[7] = bounds
            else:
                send_buf[p] = value
                meta_send[p] = bounds
                c_copies[p].start()
                m_copies[p].start()

    for copy in h_copies:
        copy.wait()
    h = h_buf[...].reshape(8 * cap, ff)
    gl_s[...] = nt_dot(h, h)
    eye = (iota((ff, ff), 0) == iota((ff, ff), 1)).astype(F32).astype(BF16)
    ht_s[...] = nt_dot(eye, h).astype(BF16)

    for p in range(7):
        m_copies[p].wait_recv()
    slot_128 = iota((cap, 128), 0).astype(F32)
    member = jnp.concatenate(
        [
            jnp.where(
                (slot_128 >= meta_recv[p, 0:1, :]) & (slot_128 < meta_recv[p, 1:2, :]), 1.0, 0.0
            )
            for p in range(8)
        ],
        axis=0,
    )
    member_b = member.astype(BF16)
    gl_s[...] = gl_s[...] * nt_dot(member_b, member_b)
    for p in range(7):
        c_copies[p].wait_recv()
    cot = c_buf[...].reshape(8 * cap, dw)
    spread = jnp.sum(gl_s[...] * nt_dot(cot, cot), axis=1, keepdims=True)
    squares = jnp.sum(member * spread, axis=0, keepdims=True)
    sq_send[...] = jnp.broadcast_to(squares, (8, 128))
    q_copies = [
        other(sq_send, sq_recv.at[p], q_send.at[p], q_recv.at[p], expert=dest[p]) for p in range(7)
    ]
    for copy in q_copies:
        copy.start()
    total = squares
    for p in range(7):
        q_copies[p].wait_recv()
        total = total + sq_recv[p, 0:1, :]
    clip = 1.0 / jnp.maximum(jnp.sqrt(total / (ff * dw)), 1.0)
    slot_weight = jnp.sum(member * clip, axis=1, keepdims=True) / EXAMPLES
    scaled_s[...] = (slot_weight * cot.astype(F32)).astype(BF16)

    rows_x = ff // NX
    t = rows_x // nz * (dw // 128)
    half = half_ring * t

    def gradient(chunk):
        start = pl.multiple_of(chunk * rows_x, 16)
        value = nn_dot(ht_s[pl.ds(start, rows_x), :], scaled_s[...])
        for j in range(dw // 128):
            acc_a[chunk, pl.ds(j, rows_x, stride=dw // 128), :] = value[:, j * 128 : (j + 1) * 128]

    lower, upper = pl.ds(0, half), pl.ds(half, half)
    gradient(x2)
    opp = [
        other(acc_a.at[x2, lower], ax_opp.at[0], ax_send.at[0], ax_recv.at[0], **at_xp),
        other(acc_a.at[x2, upper], ax_opp.at[1], ax_send.at[1], ax_recv.at[1], **at_xm),
    ]
    for copy in opp:
        copy.start()
    first = [
        other(acc_a.at[xp, upper], ax_dir.at[0, upper], ax_send.at[2], ax_recv.at[2], **at_xp),
        other(acc_a.at[xm, lower], ax_dir.at[1, lower], ax_send.at[3], ax_recv.at[3], **at_xm),
    ]
    gradient(xp)
    first[0].start()
    gradient(xm)
    first[1].start()
    gradient(x)
    second = [
        other(acc_a.at[xp, lower], ax_dir.at[0, lower], ax_send.at[4], ax_recv.at[4], **at_xp),
        other(acc_a.at[xm, upper], ax_dir.at[1, upper], ax_send.at[5], ax_recv.at[5], **at_xm),
    ]
    opp[0].wait_recv()
    acc_a[xp, lower, :] = acc_a[xp, lower, :] + ax_opp[0]
    second[0].start()
    opp[1].wait_recv()
    acc_a[xm, upper, :] = acc_a[xm, upper, :] + ax_opp[1]
    second[1].start()
    for copy in first + second:
        copy.wait_recv()
    acc_a[x] = acc_a[x] + (ax_dir[0] + ax_dir[1])

    def rows_of(d):
        return pl.ds(pl.multiple_of(d * t, 8), t)

    ring = []
    for step in range(half_ring):
        d = rows_of((z + half_ring - step) % nz)
        if step:
            ring[-1][0].wait_recv()
            acc_a[x, d, :] = acc_a[x, d, :] + azp[step - 1]
        pair = [
            other(acc_a.at[x, d], azp.at[step], azp_send.at[step], azp_recv.at[step], **at_zp)
        ]
        pair[0].start()
        if step < half_ring - 1:
            d = rows_of((z + nz - (half_ring - 1) + step) % nz)
            if step:
                ring[-1][1].wait_recv()
                acc_a[x, d, :] = acc_a[x, d, :] + azm[step - 1]
            pair.append(
                other(acc_a.at[x, d], azm.at[step], azm_send.at[step], azm_recv.at[step], **at_zm)
            )
            pair[1].start()
        ring.append(pair)
    ring[half_ring - 2][1].wait_recv()
    ring[half_ring - 1][0].wait_recv()
    out_ref[...] = acc_a[x, rows_of(z), :] + azp[half_ring - 1] + azm[half_ring - 2]
    for copy in c_copies + m_copies + q_copies + opp + first + second + [c for p in ring for c in p]:
        copy.wait_send()


def shards(nz, grad_out, routes, route_weight, example_ids, example_weight, hidden):
    tok, dw = grad_out.shape
    cap, ff = hidden.shape[3:]
    rows_x = ff // NX * (dw // 128)
    t = rows_x // nz
    half_ring = nz // 2
    dma = pltpu.SemaphoreType.DMA
    vmem = pl.BlockSpec(memory_space=pltpu.VMEM)
    scratch = [
        pltpu.VMEM((8, cap, ff), BF16),
        pltpu.VMEM((8, tok), F32),
        pltpu.VMEM((8, tok), F32),
        pltpu.VMEM((8, 128), F32),
        pltpu.VMEM((8, 128), F32),
        pltpu.VMEM((7, cap, dw), BF16),
        pltpu.VMEM((8, cap, dw), BF16),
        pltpu.VMEM((7, 8, 128), F32),
        pltpu.VMEM((8, 8, 128), F32),
        pltpu.VMEM((8, 128), F32),
        pltpu.VMEM((7, 8, 128), F32),
        pltpu.VMEM((8 * cap, 8 * cap), F32),
        pltpu.VMEM((ff, 8 * cap), BF16),
        pltpu.VMEM((8 * cap, dw), BF16),
        pltpu.VMEM((NX, rows_x, 128), F32),
        pltpu.VMEM((2, rows_x // 2, 128), F32),
        pltpu.VMEM((2, rows_x, 128), F32),
        pltpu.VMEM((half_ring, t, 128), F32),
        pltpu.VMEM((max(half_ring - 1, 1), t, 128), F32),
        dma((8,)), dma((7,)), dma((7,)), dma((7,)), dma((7,)), dma((7,)), dma((7,)),
        dma((6,)), dma((6,)), dma((half_ring,)), dma((half_ring,)), dma((half_ring,)), dma((half_ring,)),
    ]
    out = pl.pallas_call(
        functools.partial(body, (nz, ff, dw, cap, tok)),
        out_shape=jax.ShapeDtypeStruct((t, 128), F32),
        in_specs=[vmem] * 5 + [pl.BlockSpec(memory_space=pl.ANY)],
        out_specs=vmem,
        scratch_shapes=scratch,
        compiler_params=pltpu.CompilerParams(
            collective_id=0, has_side_effects=True, vmem_limit_bytes=48 * 1024 * 1024
        ),
        name="clipped_grads",
    )(grad_out, routes.T, route_weight.T, example_ids, example_weight, hidden[0, 0])
    return out.reshape(t // (dw // 128), 1, dw)


def solution(mesh):
    nz = mesh.shape["dp"] // NX
    placed = (
        P(("dp", "expert"), None),
        P(("dp", "expert"), None),
        P(("dp", "expert"), None),
        P("dp", "expert"),
        P("dp", None),
        P("dp", "expert", None, None, None),
    )
    return jax.shard_map(
        functools.partial(shards, nz), mesh=mesh, in_specs=placed,
        out_specs=P("dp", "expert", None), check_vma=False,
    )
```

time: 383 us -> 86.8 us (0.23)
  waiting for transfers between devices: 284 us -> 0 us
  Pallas kernels: 0 us -> 80.5 us
  blocking collectives: 37.5 us -> 0 us
  matrix products: 19.7 us -> 0 us
  between operations: 14.2 us -> 0.02 us
  starting transfers between devices: 9.05 us -> 0 us
  local copies, waits for them, and re-layouts: 13.3 us -> 4.8 us
  other arithmetic: 4.01 us -> 0 us
    unnamed x2 -> x0, waiting for transfers between devices: 284 us -> none
    pallas_call x0 -> x1, Pallas kernels: none -> 80.5 us  [shards(): pl.pallas_call(functools.partial(body, (nz, ff, dw, cap, tok)), out_shape...]
    all_gather x2 -> x0, blocking collectives: 25.6 us -> none  [the longest x1 17.8 us: shards(): lax.all_gather(routes, 'expert', axis=0, tiled=True)]
    dot_general x11 -> x0, matrix products: 19.7 us -> none  [the longest x8 15.9 us: shards(): jnp.einsum('jif,jid->jfd', acts_slots, chosen, preferred_element_type=jnp...]
    psum x1 -> x0, blocking collectives: 11.9 us -> none  [shards(): total_squares = lax.psum(squares, 'expert')]
    all_to_all x1 -> x0, starting transfers between devices: 9.05 us -> none  [shards(): lax.all_to_all(outgoing, 'expert', split_axis=0, concat_axis=0, tiled=True)]
    another operation x4 -> x0, local copies, waits for them, and re-layouts: 5.18 us -> none  [the longest x1 5.02 us: shards(): squares = jnp.stack(pieces)]
    transpose x2 -> x0, local copies, waits for them, and re-layouts: 4.6 us -> none  [the longest x1 4.58 us: shards(): jnp.einsum('jif,jid->fjd', acts_slots, scaled, preferred_element_type=jnp...]
  transfers between devices with their start and end apart: 2 -> 0, of which waited for: 1 -> 0; matrix products, arithmetic and copies ran while one was open for 1% -> 0% of each run, Pallas kernels for 0% -> 0%
where the time goes in v1:
time: 86.8 us; the launch traced here: 85.3 us
  Pallas kernels  80.5 us (93%)
  local copies, waits for them, and re-layouts  4.8 us (6%)
    pallas_call x1, Pallas kernels, shards(): pl.pallas_call(functools.partial(body, (nz, ff, dw, cap, tok)), out_shape...  80.5 us
    unnamed x13, local copies, waits for them, and re-layouts  4.8 us

profile of v1, /device:TPU:24, one launch (start us, length us, event | category | flops | bytes accessed | tf_op | source)
XLA Modules:
  0.0 85.3 jit_solution(4797840592920434188)
XLA Ops:
  0.0 0.0 copy-start.4
  0.0 0.0 copy-start.5
  0.0 0.7 copy-done.4
  0.7 0.0 copy-done.5
  0.7 0.0 copy-start
  0.7 1.1 %copy-done = bf16[1,1,8,48,704]{4,3,2,1,0:T(8,128)(2,1)S(1)} copy-done((bf16[1,1,8,48,704]{4,3,2,1,0:T(8,128)(2,1)S(1)}, bf16[1,1,8,48,704]{4,3,2,1,0:T(8,128)(2,1)}, u32[]{:S(2)}) %copy-start) | copy-done | bytes 540696
  1.7 0.0 copy-start.1
  1.8 1.0 %copy-done.1 = bf16[256,1024]{1,0:T(8,128)(2,1)S(1)} copy-done((bf16[256,1024]{1,0:T(8,128)(2,1)S(1)}, bf16[256,1024]{1,0:T(8,128)(2,1)}, u32[]{:S(2)}) %copy-start.1) | copy-done | bytes 524312
  2.8 0.0 copy-start.2
  2.8 0.7 copy-done.2
  3.5 0.0 copy-start.3
  3.5 0.7 copy-done.3
  4.2 80.5 %clipped_grads.1 = f32[88,128]{1,0:T(8,128)S(1)} custom-call(bf16[256,1024]{1,0:T(8,128)(2,1)S(1)} %copy-done.1, s32[6,256]{1,0:T(8,128)S(1)} %bitcast.6, f32[6,256]{1,0:T(8,128)S(1)} %bitcast.7, s32[1,256]{1,0:T(1,128)S(1)} %copy-done.4, f32[1,8]{1,0:T(1,128)S(1)} %copy-done.5, bf16[8,48,704]{2,1,0:T(8,128)(2,1)S(1)} %bitcast.4), custom_call_target="tpu_custom_call" | custom-call | tf_op jit(solution)/shard_map/clipped_grads/pallas_call | solution.py:272
  84.7 0.6 copy.10
Async XLA Ops:
  0.0 0.7 copy-start.4
  0.0 0.7 copy-start.5
  0.7 1.1 %copy-start = (bf16[1,1,8,48,704]{4,3,2,1,0:T(8,128)(2,1)S(1)}, bf16[1,1,8,48,704]{4,3,2,1,0:T(8,128)(2,1)}, u32[]{:S(2)}) copy-start(bf16[1,1,8,48,704]{4,3,2,1,0:T(8,128)(2,1)} %param.11) | copy-start | bytes 1622020
  1.7 1.0 %copy-start.1 = (bf16[256,1024]{1,0:T(8,128)(2,1)S(1)}, bf16[256,1024]{1,0:T(8,128)(2,1)}, u32[]{:S(2)}) copy-start(bf16[256,1024]{1,0:T(8,128)(2,1)} %go_ref.1) | copy-start | bytes 1572868
  2.8 0.7 copy-start.2
  3.5 0.7 copy-start.3

commit v2 on v1

v2 whole, which is shorter than its diff:
```python
import functools

import jax
import jax.numpy as jnp
from jax import lax
from jax.experimental import pallas as pl
from jax.experimental.pallas import tpu as pltpu
from jax.sharding import PartitionSpec as P

EXAMPLES = 8
TOP = 6
NX = 4
MESH = pl.DeviceIdType.MESH
F32 = jnp.float32
BF16 = jnp.bfloat16

X_FIRST = 6
LINKS = 112

REL = ((2, 0), (2, 1), (1, 0), (3, 0), (1, 1), (3, 1), (0, 1), (0, 0))


def nt_dot(a, b):
    return lax.dot_general(a, b, (((1,), (1,)), ((), ())), preferred_element_type=F32)


def nn_dot(a, b):
    return lax.dot_general(a, b, (((1,), (0,)), ((), ())), preferred_element_type=F32)


def iota(shape, dim):
    return lax.broadcasted_iota(jnp.int32, shape, dim)


def other(src, dst, send_sem, recv_sem, **device):
    return pltpu.make_async_remote_copy(
        src_ref=src, dst_ref=dst, send_sem=send_sem, recv_sem=recv_sem,
        device_id=device, device_id_type=MESH,
    )


def encode(value):
    most = jnp.max(jnp.abs(value), axis=0, keepdims=True)
    step = jnp.maximum(most, 1e-33) * (1.0 / 32760.0)
    code = jnp.round(value * (1.0 / step)).astype(jnp.int32)
    return code, jnp.broadcast_to(step, (8, 128))


def decode(code, step):
    return code.astype(jnp.int32).astype(F32) * step


def body(
    cfg,
    go_hbm, routes_hbm, weight_hbm, ids_hbm, ew_hbm, h_ref,
    out_ref,
    go_ref, routes_ref, weight_ref, ids_ref, ew_ref,
    h_buf, rank_s, scale_s, lo_s, hi_s, send_buf, relay_buf, c_buf, meta_send, meta_recv, sq_send, sq_recv,
    gl_s, ht_s, scaled_s,
    acc_a, acc_b, x_codes, x_steps, x_in, x_in_steps,
    za_codes, za_in, zb_codes, zb_in, za2_codes, za2_in, zb2_codes, zb2_in,
    z_steps, z_in_steps, bx_codes, bx_in, bx_steps,
    local_sem, send_sem, recv_sem,
):
    nz, ff, dw, cap, tok = cfg
    lanes = dw // 128
    dp, me = lax.axis_index("dp"), lax.axis_index("expert")
    x, z = dp // nz, dp % nz
    y, core = me // 2, me % 2
    xp, xm, x2 = (x + 1) % NX, (x + 3) % NX, (x + 2) % NX

    def expert_at(dy, dc):
        return dict(expert=((y + dy) % 4) * 2 + (core + dc) % 2)

    def x_at(dx):
        return dict(dp=((x + dx) % NX) * nz + z)

    def z_at(dz):
        return dict(dp=x * nz + (z + nz + dz) % nz)

    dest = [expert_at(dy, dc)["expert"] for dy, dc in REL]
    source = [((y + 4 - dy) % 4) * 2 + (core + 2 - dc) % 2 for dy, dc in REL]
    copies = []

    def link(src, dst, place):
        n = len(copies)
        copies.append(other(src, dst, send_sem.at[n], recv_sem.at[n], **place))
        return copies[-1]

    barrier = pltpu.get_barrier_semaphore()
    greeted = [expert_at(dy, dc) for dy, dc in REL[:7]]
    greeted += [x_at(dx) for dx in (1, 2, 3)] + [z_at(dz) for dz in (1, -1, 2, -2, 3, -3, 5, -5)]
    for place in greeted:
        pl.semaphore_signal(barrier, inc=1, device_id=place, device_id_type=MESH)

    inputs = [
        pltpu.make_async_copy(src, dst, local_sem.at[n])
        for n, (src, dst) in enumerate((
            (routes_hbm, routes_ref), (weight_hbm, weight_ref), (ids_hbm, ids_ref),
            (ew_hbm, ew_ref), (go_hbm, go_ref),
        ))
    ]
    for copy in inputs:
        copy.start()
    h_copies = [
        pltpu.make_async_copy(h_ref.at[source[p]], h_buf.at[p], local_sem.at[5 + p])
        for p in range(8)
    ]
    for copy in h_copies:
        copy.start()
    for copy in inputs[:4]:
        copy.wait()

    expert_row = iota((8, tok), 0)
    routed = jnp.zeros((8, tok), F32)
    weight = jnp.zeros((8, tok), F32)
    for k in range(TOP):
        match = routes_ref[k : k + 1, :] == expert_row
        routed = jnp.where(match, 1.0, routed)
        weight = jnp.where(match, weight_ref[k : k + 1, :], weight)
    ids = ids_ref[...]
    token_weight = jnp.zeros((1, tok), F32)
    for example in range(EXAMPLES):
        token_weight = jnp.where(
            ids == example, ew_ref[0:1, example : example + 1], token_weight
        )
    earlier = (iota((tok, tok), 0) < iota((tok, tok), 1)).astype(F32).astype(BF16)
    routed_b = routed.astype(BF16)
    rank = nn_dot(routed_b, earlier)
    rank_s[...] = jnp.where(routed > 0.5, rank, -1.0)
    scale_s[...] = weight * token_weight
    example_col = iota((128, tok), 0)
    lo_s[...] = nt_dot(routed_b, (ids < example_col).astype(F32).astype(BF16))
    hi_s[...] = nt_dot(routed_b, (ids <= example_col).astype(F32).astype(BF16))

    slot_col = iota((cap, tok), 0).astype(F32)
    sub8 = iota((8, 128), 0)
    c_copies = [
        link(send_buf.at[0], relay_buf.at[0], expert_at(1, 0)),
        link(send_buf.at[1], relay_buf.at[1], expert_at(3, 0)),
    ]
    c_copies += [link(send_buf.at[p], c_buf.at[p], expert_at(*REL[p])) for p in range(2, 7)]
    relays = [
        link(relay_buf.at[0], c_buf.at[0], expert_at(1, 0)),
        link(relay_buf.at[1], c_buf.at[1], expert_at(3, 1)),
    ]
    m_copies = [link(meta_send.at[p], meta_recv.at[p], expert_at(*REL[p])) for p in range(7)]
    inputs[4].wait()
    for batch in ((0, 1), (2, 3, 4, 5), (6, 7)):
        masks, scales = [], []
        for p in batch:
            hit = rank_s[pl.ds(dest[p], 1), :] == slot_col
            masks.append(hit.astype(F32).astype(BF16))
            scales.append(
                jnp.sum(jnp.where(hit, scale_s[pl.ds(dest[p], 1), :], 0.0), axis=1, keepdims=True)
            )
        rows = nn_dot(jnp.concatenate(masks, axis=0), go_ref[...])
        if batch[0] == 0:
            pl.semaphore_wait(barrier, len(greeted))
        for i, p in enumerate(batch):
            value = (rows[i * cap : (i + 1) * cap, :] * scales[i]).astype(BF16)
            bounds = jnp.where(
                sub8 == 0, lo_s[pl.ds(dest[p], 1), :], hi_s[pl.ds(dest[p], 1), :]
            )
            if p == 7:
                c_buf[7] = value
                meta_recv[7] = bounds
            else:
                send_buf[p] = value
                meta_send[p] = bounds
                c_copies[p].start()
                m_copies[p].start()

    for copy in h_copies:
        copy.wait()
    h = h_buf[...].reshape(8 * cap, ff)
    gl_s[...] = nt_dot(h, h)
    share = ff // (NX * nz)
    na = X_FIRST
    nb = share - na
    split = NX * nz * na
    j = iota((ff, 1), 0).astype(F32)
    qa = jnp.floor((j + 0.5) * (1.0 / na))
    unit_a = share * qa + (j - na * qa)
    jb = j - split
    qb = jnp.floor((jb + 0.5) * (1.0 / nb))
    zb = jnp.floor((qb + 0.5) * (1.0 / NX))
    unit_b = share * (nz * (qb - NX * zb) + zb) + na + (jb - nb * qb)
    unit = jnp.where(j < split, unit_a, unit_b)
    order = (iota((ff, ff), 1).astype(F32) == unit).astype(F32).astype(BF16)
    ht_s[...] = nt_dot(order, h).astype(BF16)

    for n in range(2):
        c_copies[n].wait_recv()
        relays[n].start()
    for p in range(7):
        m_copies[p].wait_recv()
    slot_128 = iota((cap, 128), 0).astype(F32)
    member = jnp.concatenate(
        [
            jnp.where(
                (slot_128 >= meta_recv[p, 0:1, :]) & (slot_128 < meta_recv[p, 1:2, :]), 1.0, 0.0
            )
            for p in range(8)
        ],
        axis=0,
    )
    member_b = member.astype(BF16)
    gl_s[...] = gl_s[...] * nt_dot(member_b, member_b)
    for p in range(2, 7):
        c_copies[p].wait_recv()
    for copy in relays:
        copy.wait_recv()
    cot = c_buf[...].reshape(8 * cap, dw)
    spread = jnp.sum(gl_s[...] * nt_dot(cot, cot), axis=1, keepdims=True)
    squares = jnp.sum(member * spread, axis=0, keepdims=True)
    sq_send[...] = jnp.broadcast_to(squares, (8, 128))
    q_copies = [link(sq_send, sq_recv.at[p], expert_at(*REL[p])) for p in range(7)]
    for copy in q_copies:
        copy.start()
    total = squares
    for p in range(7):
        q_copies[p].wait_recv()
        total = total + sq_recv[p, 0:1, :]
    clip = 1.0 / jnp.maximum(jnp.sqrt(total / (ff * dw)), 1.0)
    slot_weight = jnp.sum(member * clip, axis=1, keepdims=True) / EXAMPLES
    scaled_s[...] = (slot_weight * cot.astype(F32)).astype(BF16)

    ra, rb = na * lanes, nb * lanes
    rows_a = nz * na
    half = nz // 2

    def gradient_a(chunk):
        value = nn_dot(ht_s[pl.ds(pl.multiple_of(chunk * rows_a, 16), rows_a), :], scaled_s[...])
        for n in range(lanes):
            acc_a[chunk, pl.ds(n, rows_a, stride=lanes), :] = value[:, n * 128 : (n + 1) * 128]

    def coded(value, count, rows):
        code, step = encode(value)
        return code.reshape(count, rows, 128).astype(jnp.int16), step

    lower, upper = pl.ds(0, half * ra), pl.ds(half * ra, half * ra)

    def x_message(n, place):
        return [
            link(x_codes.at[n], x_in.at[n], place), link(x_steps.at[n], x_in_steps.at[n], place)
        ]

    def x_send(n, value, message):
        x_codes[n], x_steps[n] = coded(value, half, ra)
        for copy in message:
            copy.start()

    def x_value(n):
        return decode(x_in[n], x_in_steps[n, 0:1, :]).reshape(half * ra, 128)

    messages = [x_message(n, x_at(1 if n % 2 == 0 else 3)) for n in range(6)]
    gradient_a(x2)
    x_send(0, acc_a[x2, lower, :], messages[0])
    x_send(1, acc_a[x2, upper, :], messages[1])
    gradient_a(xp)
    x_send(2, acc_a[xp, upper, :], messages[2])
    gradient_a(xm)
    x_send(3, acc_a[xm, lower, :], messages[3])

    value = nn_dot(ht_s[split:, :], scaled_s[...])
    for n in range(lanes):
        acc_b[pl.ds(n, NX * nz * nb, stride=lanes), :] = value[:, n * 128 : (n + 1) * 128]

    def z_start(which, sums, rows, codes, taken, side):
        codes[...], z_steps[which] = coded(sums, nz, rows)
        started = []
        near = ((2, 0), (-2, 1), (1, 2), (-1, 3))
        plan = [(o, n, ((0, 0), (5, 1), (-5, 2))) for o, n in near]
        plan.insert(2, (3 * side, 4, ((5 * side, 0),)))
        for o, n, wanted in plan:
            started.append(link(z_steps.at[which], z_in_steps.at[which, n], z_at(o)))
            for d, m in wanted:
                started.append(
                    link(codes.at[(z + nz + o + d) % nz], taken.at[3 * n + m], z_at(o))
                )
        for copy in started:
            copy.start()
        return started

    def z_middle(which, started, sums_at, rows, taken, codes, taken2, side):
        for copy in started:
            copy.wait_recv()
        pieces = [sums_at(z), sums_at((z + 5) % nz), sums_at((z + nz - 5) % nz)]
        for n in range(4):
            for m in range(3):
                pieces[m] = pieces[m] + decode(taken[3 * n + m], z_in_steps[which, n, 0:1, :])
        far = 1 if side == 1 else 2
        pieces[far] = pieces[far] + decode(taken[12], z_in_steps[which, 4, 0:1, :])
        codes[...], z_steps[2 + which] = coded(jnp.concatenate(pieces[1:], axis=0), 2, rows)
        started = []
        for n, o in enumerate((5, -5)):
            started.append(link(z_steps.at[2 + which], z_in_steps.at[which, 5 + n], z_at(o)))
            started.append(link(codes.at[n], taken2.at[n], z_at(o)))
        for copy in started:
            copy.start()
        return pieces[0], started

    def z_end(which, value, started, taken2):
        for copy in started:
            copy.wait_recv()
        for n in range(2):
            value = value + decode(taken2[n], z_in_steps[which, 5 + n, 0:1, :])
        return value

    def a_at(d):
        return acc_a[x, pl.ds(pl.multiple_of(d * ra, 8), ra), :]

    def b_at(d):
        return acc_b[pl.ds(pl.multiple_of(d * NX * rb, 8), NX * rb), :]

    b_started = z_start(1, acc_b[...], NX * rb, zb_codes, zb_in, -1)
    gradient_a(x)
    for n, chunk, part in ((4, xp, lower), (5, xm, upper)):
        for copy in messages[n - 4]:
            copy.wait_recv()
        x_send(n, acc_a[chunk, part, :] + x_value(n - 4), messages[n])
    for n in (2, 3, 4, 5):
        for copy in messages[n]:
            copy.wait_recv()
    acc_a[x, lower, :] = acc_a[x, lower, :] + (x_value(4) + x_value(3))
    acc_a[x, upper, :] = acc_a[x, upper, :] + (x_value(2) + x_value(5))
    a_started = z_start(0, acc_a[x], ra, za_codes, za_in, 1)
    b_sum, b_started = z_middle(1, b_started, b_at, NX * rb, zb_in, zb2_codes, zb2_in, -1)
    a_sum, a_started = z_middle(0, a_started, a_at, ra, za_in, za2_codes, za2_in, 1)
    b_sum = z_end(1, b_sum, b_started, zb2_in)
    bx_codes[...], bx_steps[0] = coded(b_sum, NX, rb)
    acc_b[pl.ds(0, NX * rb), :] = b_sum
    last = []
    for n, dx in enumerate((2, 1, 3)):
        last.append(link(bx_steps.at[0], bx_steps.at[1 + n], x_at(dx)))
        last.append(link(bx_codes.at[(x + dx) % NX], bx_in.at[n], x_at(dx)))
    for copy in last:
        copy.start()
    out_ref[0:ra, :] = z_end(0, a_sum, a_started, za2_in)
    value = acc_b[pl.ds(pl.multiple_of(x * rb, 8), rb), :]
    for copy in last:
        copy.wait_recv()
    for n in range(3):
        value = value + decode(bx_in[n], bx_steps[1 + n, 0:1, :])
    out_ref[ra:, :] = value
    for copy in copies:
        copy.wait_send()


def shards(nz, grad_out, routes, route_weight, example_ids, example_weight, hidden):
    tok, dw = grad_out.shape
    cap, ff = hidden.shape[3:]
    lanes = dw // 128
    share = ff // (NX * nz)
    ra, rb = X_FIRST * lanes, (share - X_FIRST) * lanes
    half = nz // 2
    i16 = jnp.int16
    dma = pltpu.SemaphoreType.DMA
    scratch = [
        pltpu.VMEM((tok, dw), BF16),
        pltpu.VMEM((TOP, tok), jnp.int32),
        pltpu.VMEM((TOP, tok), F32),
        pltpu.VMEM((1, tok), jnp.int32),
        pltpu.VMEM((1, EXAMPLES), F32),
        pltpu.VMEM((8, cap, ff), BF16),
        pltpu.VMEM((8, tok), F32),
        pltpu.VMEM((8, tok), F32),
        pltpu.VMEM((8, 128), F32),
        pltpu.VMEM((8, 128), F32),
        pltpu.VMEM((7, cap, dw), BF16),
        pltpu.VMEM((2, cap, dw), BF16),
        pltpu.VMEM((8, cap, dw), BF16),
        pltpu.VMEM((7, 8, 128), F32),
        pltpu.VMEM((8, 8, 128), F32),
        pltpu.VMEM((8, 128), F32),
        pltpu.VMEM((7, 8, 128), F32),
        pltpu.VMEM((8 * cap, 8 * cap), F32),
        pltpu.VMEM((ff, 8 * cap), BF16),
        pltpu.VMEM((8 * cap, dw), BF16),
        pltpu.VMEM((NX, nz * ra, 128), F32),
        pltpu.VMEM((nz * NX * rb, 128), F32),
        pltpu.VMEM((6, half, ra, 128), i16),
        pltpu.VMEM((6, 8, 128), F32),
        pltpu.VMEM((6, half, ra, 128), i16),
        pltpu.VMEM((6, 8, 128), F32),
        pltpu.VMEM((nz, ra, 128), i16),
        pltpu.VMEM((13, ra, 128), i16),
        pltpu.VMEM((nz, NX * rb, 128), i16),
        pltpu.VMEM((13, NX * rb, 128), i16),
        pltpu.VMEM((2, ra, 128), i16),
        pltpu.VMEM((2, ra, 128), i16),
        pltpu.VMEM((2, NX * rb, 128), i16),
        pltpu.VMEM((2, NX * rb, 128), i16),
        pltpu.VMEM((4, 8, 128), F32),
        pltpu.VMEM((2, 7, 8, 128), F32),
        pltpu.VMEM((NX, rb, 128), i16),
        pltpu.VMEM((3, rb, 128), i16),
        pltpu.VMEM((4, 8, 128), F32),
        dma((13,)), dma((LINKS,)), dma((LINKS,)),
    ]
    out = pl.pallas_call(
        functools.partial(body, (nz, ff, dw, cap, tok)),
        out_shape=jax.ShapeDtypeStruct((share * lanes, 128), F32),
        in_specs=[pl.BlockSpec(memory_space=pl.ANY)] * 6,
        out_specs=pl.BlockSpec(memory_space=pltpu.VMEM),
        scratch_shapes=scratch,
        compiler_params=pltpu.CompilerParams(
            collective_id=0, has_side_effects=True, vmem_limit_bytes=62 * 1024 * 1024
        ),
        name="clipped_grads",
    )(grad_out, routes.T, route_weight.T, example_ids, example_weight, hidden[0, 0])
    return out.reshape(share, 1, dw)


def solution(mesh):
    nz = mesh.shape["dp"] // NX
    placed = (
        P(("dp", "expert"), None),
        P(("dp", "expert"), None),
        P(("dp", "expert"), None),
        P("dp", "expert"),
        P("dp", None),
        P("dp", "expert", None, None, None),
    )
    return jax.shard_map(
        functools.partial(shards, nz), mesh=mesh, in_specs=placed,
        out_specs=P("dp", "expert", None), check_vma=False,
    )
```

time: 86.8 us -> 61.8 us (0.71); the launches traced: 85.3 us -> 61.3 us
  Pallas kernels: 80.5 us -> 59.9 us
  local copies, waits for them, and re-layouts: 4.8 us -> 1.41 us
    pallas_call x1, Pallas kernels: 80.5 us -> 59.9 us  [shards(): pl.pallas_call(functools.partial(body, (nz, ff, dw, cap, tok)), out_shape...]
    unnamed x13 -> x1, local copies, waits for them, and re-layouts: 4.8 us -> 1.41 us
where the time goes in v2:
time: 61.8 us; the launch traced here: 61.3 us
  Pallas kernels  59.9 us (97%)
  local copies, waits for them, and re-layouts  1.41 us (2%)
    pallas_call x1, Pallas kernels, shards(): pl.pallas_call(functools.partial(body, (nz, ff, dw, cap, tok)), out_shape...  59.9 us
    unnamed x1, local copies, waits for them, and re-layouts  1.41 us

profile of v2, /device:TPU:24, one launch (start us, length us, event | category | flops | bytes accessed | tf_op | source)
XLA Modules:
  0.0 61.3 jit_solution(4765367628366176007)
XLA Ops:
  0.0 59.9 %clipped_grads.1 = f32[88,128]{1,0:T(8,128)} custom-call(bf16[256,1024]{1,0:T(8,128)(2,1)} %go_hbm.1, s32[6,256]{1,0:T(8,128)} %bitcast.6, f32[6,256]{1,0:T(8,128)} %bitcast.7, s32[1,256]{1,0:T(1,128)} %ids_hbm.1, f32[1,8]{1,0:T(1,128)} %ew_hbm.1, bf16[8,48,704]{2,1,0:T(8,128)(2,1)} %bitcast.4), custom_call_target="tpu_custom_call" | custom-call | tf_op jit(solution)/shard_map/clipped_grads/pallas_call | solution.py:402
  59.9 1.4 %copy.10 = f32[11,1,1024]{2,1,0:T(1,128)} copy(f32[11,1,1024]{2,1,0:T(1,128)} %bitcast.5) | data formatting | bytes 90112

commit v3 on v2

v3 whole, which is shorter than its diff:
```python
import functools

import jax
import jax.numpy as jnp
from jax import lax
from jax.experimental import pallas as pl
from jax.experimental.pallas import tpu as pltpu
from jax.sharding import PartitionSpec as P

EXAMPLES = 8
TOP = 6
NX = 4
MESH = pl.DeviceIdType.MESH
F32 = jnp.float32
BF16 = jnp.bfloat16

RUNS = (4, 3)
LINKS = 128

REL = ((2, 0), (2, 1), (1, 0), (3, 0), (1, 1), (3, 1), (0, 1), (0, 0))


def nt_dot(a, b):
    return lax.dot_general(a, b, (((1,), (1,)), ((), ())), preferred_element_type=F32)


def nn_dot(a, b):
    return lax.dot_general(a, b, (((1,), (0,)), ((), ())), preferred_element_type=F32)


def iota(shape, dim):
    return lax.broadcasted_iota(jnp.int32, shape, dim)


def other(src, dst, send_sem, recv_sem, **device):
    return pltpu.make_async_remote_copy(
        src_ref=src, dst_ref=dst, send_sem=send_sem, recv_sem=recv_sem,
        device_id=device, device_id_type=MESH,
    )


def encode(value):
    most = jnp.max(jnp.abs(value), axis=0, keepdims=True)
    step = jnp.maximum(most, 1e-33) * (1.0 / 32760.0)
    code = jnp.round(value * (1.0 / step)).astype(jnp.int32)
    return code, step


def decode(code, step):
    return code.astype(jnp.int32).astype(F32) * step


def body(
    cfg,
    go_hbm, routes_hbm, weight_hbm, ids_hbm, ew_hbm, h_ref,
    out_ref,
    go_ref, routes_ref, weight_ref, ids_ref, ew_ref,
    h_buf, rank_s, scale_s, lo_s, hi_s, send_buf, relay_buf, c_buf, meta_send, meta_recv, sq_send, sq_recv,
    gl_s, ht_s, scaled_s, parts,
    local_sem, send_sem, recv_sem,
):
    nz, ff, dw, cap, tok = cfg
    lanes = dw // 128
    dp, me = lax.axis_index("dp"), lax.axis_index("expert")
    x, z = dp // nz, dp % nz
    y, core = me // 2, me % 2
    xp, xm, x2 = (x + 1) % NX, (x + 3) % NX, (x + 2) % NX

    def expert_at(dy, dc):
        return dict(expert=((y + dy) % 4) * 2 + (core + dc) % 2)

    def x_at(dx):
        return dict(dp=((x + dx) % NX) * nz + z)

    def z_at(dz):
        return dict(dp=x * nz + (z + nz + dz) % nz)

    dest = [expert_at(dy, dc)["expert"] for dy, dc in REL]
    source = [((y + 4 - dy) % 4) * 2 + (core + 2 - dc) % 2 for dy, dc in REL]
    copies = []

    def link(src, dst, place):
        n = len(copies)
        copies.append(other(src, dst, send_sem.at[n], recv_sem.at[n], **place))
        return copies[-1]

    barrier = pltpu.get_barrier_semaphore()
    greeted = [expert_at(dy, dc) for dy, dc in REL[:7]]
    greeted += [x_at(dx) for dx in (1, 2, 3)] + [z_at(dz) for dz in (1, -1, 2, -2, 3, -3)]
    for place in greeted:
        pl.semaphore_signal(barrier, inc=1, device_id=place, device_id_type=MESH)

    inputs = [
        pltpu.make_async_copy(src, dst, local_sem.at[n])
        for n, (src, dst) in enumerate((
            (routes_hbm, routes_ref), (weight_hbm, weight_ref), (ids_hbm, ids_ref),
            (ew_hbm, ew_ref), (go_hbm, go_ref),
        ))
    ]
    for copy in inputs:
        copy.start()
    h_copies = [
        pltpu.make_async_copy(h_ref.at[source[p]], h_buf.at[p], local_sem.at[5 + p])
        for p in range(8)
    ]
    for copy in h_copies:
        copy.start()
    for copy in inputs[:4]:
        copy.wait()

    expert_row = iota((8, tok), 0)
    routed = jnp.zeros((8, tok), F32)
    weight = jnp.zeros((8, tok), F32)
    for k in range(TOP):
        match = routes_ref[k : k + 1, :] == expert_row
        routed = jnp.where(match, 1.0, routed)
        weight = jnp.where(match, weight_ref[k : k + 1, :], weight)
    ids = ids_ref[...]
    token_weight = jnp.zeros((1, tok), F32)
    for example in range(EXAMPLES):
        token_weight = jnp.where(
            ids == example, ew_ref[0:1, example : example + 1], token_weight
        )
    earlier = (iota((tok, tok), 0) < iota((tok, tok), 1)).astype(F32).astype(BF16)
    routed_b = routed.astype(BF16)
    rank = nn_dot(routed_b, earlier)
    rank_s[...] = jnp.where(routed > 0.5, rank, -1.0)
    scale_s[...] = weight * token_weight
    example_col = iota((128, tok), 0)
    lo_s[...] = nt_dot(routed_b, (ids < example_col).astype(F32).astype(BF16))
    hi_s[...] = nt_dot(routed_b, (ids <= example_col).astype(F32).astype(BF16))

    slot_col = iota((cap, tok), 0).astype(F32)
    sub2 = iota((2, 128), 0)
    c_copies = [
        link(send_buf.at[0], relay_buf.at[0], expert_at(1, 0)),
        link(send_buf.at[1], relay_buf.at[1], expert_at(3, 0)),
    ]
    c_copies += [link(send_buf.at[p], c_buf.at[p], expert_at(*REL[p])) for p in range(2, 7)]
    relays = [
        link(relay_buf.at[0], c_buf.at[0], expert_at(1, 0)),
        link(relay_buf.at[1], c_buf.at[1], expert_at(3, 1)),
    ]
    m_copies = [link(meta_send.at[p], meta_recv.at[p], expert_at(*REL[p])) for p in range(7)]
    inputs[4].wait()
    for batch in ((0, 1), (2, 3, 4, 5), (6, 7)):
        masks, scales = [], []
        for p in batch:
            hit = rank_s[pl.ds(dest[p], 1), :] == slot_col
            masks.append(hit.astype(F32).astype(BF16))
            scales.append(
                jnp.sum(jnp.where(hit, scale_s[pl.ds(dest[p], 1), :], 0.0), axis=1, keepdims=True)
            )
        rows = nn_dot(jnp.concatenate(masks, axis=0), go_ref[...])
        if batch[0] == 0:
            pl.semaphore_wait(barrier, len(greeted))
        for i, p in enumerate(batch):
            value = (rows[i * cap : (i + 1) * cap, :] * scales[i]).astype(BF16)
            bounds = jnp.where(
                sub2 == 0, lo_s[pl.ds(dest[p], 1), :], hi_s[pl.ds(dest[p], 1), :]
            )
            if p == 7:
                c_buf[7] = value
                meta_recv[7] = bounds
            else:
                send_buf[p] = value
                meta_send[p] = bounds
                c_copies[p].start()
                m_copies[p].start()

    for copy in h_copies:
        copy.wait()
    h = h_buf[...].reshape(8 * cap, ff)
    gl_s[...] = nt_dot(h, h)
    share = ff // (NX * nz)
    j = iota((ff, 1), 0).astype(F32)
    unit, start, taken = j, 0, 0
    starts = []
    for n, rows in enumerate(RUNS + (share - sum(RUNS),)):
        at = j - start
        q = jnp.floor((at + 0.5) * (1.0 / rows))
        r = at - rows * q
        if n == len(RUNS):
            zq = jnp.floor((q + 0.5) * (1.0 / NX))
            q = nz * (q - NX * zq) + zq
        unit = jnp.where(j >= start, share * q + taken + r, unit)
        starts.append(start)
        start, taken = start + NX * nz * rows, taken + rows
    order = (iota((ff, ff), 1).astype(F32) == unit).astype(F32).astype(BF16)
    ht_s[...] = nt_dot(order, h).astype(BF16)

    for n in range(2):
        c_copies[n].wait_recv()
        relays[n].start()
    for p in range(7):
        m_copies[p].wait_recv()
    slot_128 = iota((cap, 128), 0).astype(F32)
    member = jnp.concatenate(
        [
            jnp.where(
                (slot_128 >= meta_recv[p, 0:1, :]) & (slot_128 < meta_recv[p, 1:2, :]), 1.0, 0.0
            )
            for p in range(8)
        ],
        axis=0,
    )
    member_b = member.astype(BF16)
    gl_s[...] = gl_s[...] * nt_dot(member_b, member_b)
    for p in range(2, 7):
        c_copies[p].wait_recv()
    for copy in relays:
        copy.wait_recv()
    cot = c_buf[...].reshape(8 * cap, dw)
    spread = jnp.sum(gl_s[...] * nt_dot(cot, cot), axis=1, keepdims=True)
    squares = jnp.sum(member * spread, axis=0, keepdims=True)
    sq_send[...] = squares
    q_copies = [link(sq_send, sq_recv.at[p], expert_at(*REL[p])) for p in range(7)]
    for copy in q_copies:
        copy.start()
    total = squares
    for p in range(7):
        q_copies[p].wait_recv()
        total = total + sq_recv[p]
    clip = 1.0 / jnp.maximum(jnp.sqrt(total / (ff * dw)), 1.0)
    slot_weight = jnp.sum(member * clip, axis=1, keepdims=True) / EXAMPLES
    scaled_s[...] = (slot_weight * cot.astype(F32)).astype(BF16)

    half = nz // 2

    def begin(messages):
        for copy in messages:
            copy.start()

    def arrive(messages):
        for copy in messages:
            copy.wait_recv()

    def gradient(dst, start, rows):
        value = nn_dot(ht_s[pl.ds(start, rows), :], scaled_s[...])
        for n in range(lanes):
            dst[pl.ds(n, rows, stride=lanes), :] = value[:, n * 128 : (n + 1) * 128]

    class AlongX:
        def __init__(self, n):
            self.start, self.rows = starts[n], nz * RUNS[n]
            self.chunk = RUNS[n] * lanes
            self.half = half * self.chunk
            self.lower, self.upper = pl.ds(0, self.half), pl.ds(self.half, self.half)
            refs = parts[n]
            self.sums, self.z = refs["sums"], refs["z"]
            self.codes, self.steps = refs["x_codes"], refs["x_steps"]
            self.taken, self.taken_steps = refs["x_in"], refs["x_in_steps"]
            self.messages = []
            for m in range(6):
                place = x_at(1 if m % 2 == 0 else 3)
                self.messages.append([
                    link(self.steps.at[m], self.taken_steps.at[m], place),
                    link(self.codes.at[m], self.taken.at[m], place),
                ])

        def gradient(self, quarter):
            start = pl.multiple_of(self.start + quarter * self.rows, 16)
            gradient(self.sums.at[quarter], start, self.rows)

        def send(self, m, value):
            code, self.steps[m] = encode(value)
            self.codes[m] = code.astype(jnp.int16)
            begin(self.messages[m])

        def value(self, m):
            return decode(self.taken[m], self.taken_steps[m])

        def opposite(self):
            self.gradient(x2)
            self.send(0, self.sums[x2, self.lower, :])
            self.send(1, self.sums[x2, self.upper, :])

        def near(self):
            self.gradient(xp)
            self.send(2, self.sums[xp, self.upper, :])
            self.gradient(xm)
            self.send(3, self.sums[xm, self.lower, :])

        def relay(self):
            arrive(self.messages[0])
            self.send(4, self.sums[xp, self.lower, :] + self.value(0))
            arrive(self.messages[1])
            self.send(5, self.sums[xm, self.upper, :] + self.value(1))

        def finish(self):
            for m in (2, 3, 4, 5):
                arrive(self.messages[m])
            self.sums[x, self.lower, :] = self.sums[x, self.lower, :] + (self.value(4) + self.value(3))
            self.sums[x, self.upper, :] = self.sums[x, self.upper, :] + (self.value(2) + self.value(5))

        def at(self, d):
            return self.sums[x, pl.ds(pl.multiple_of(d * self.chunk, 8), self.chunk), :]

    def z_start(refs, sums, rows, side):
        code, refs["steps"][0] = encode(sums)
        refs["codes"][...] = code.reshape(nz, rows, 128).astype(jnp.int16)
        plan = [(o, n, ((0, 0), (5, 1), (-5, 2))) for o, n in ((2, 0), (-2, 1), (1, 2), (-1, 3))]
        plan.insert(2, (3 * side, 4, ((5 * side, 0),)))
        started = []
        for o, n, wanted in plan:
            started.append(link(refs["steps"].at[0], refs["in_steps"].at[n], z_at(o)))
            for d, m in wanted:
                started.append(
                    link(refs["codes"].at[(z + nz + o + d) % nz], refs["in"].at[3 * n + m], z_at(o))
                )
        begin(started)
        return started

    def z_middle(refs, started, sums_at, side):
        arrive(started)
        pieces = [sums_at(z), sums_at((z + 5) % nz), sums_at((z + nz - 5) % nz)]
        for n in range(4):
            for m in range(3):
                pieces[m] = pieces[m] + decode(refs["in"][3 * n + m], refs["in_steps"][n])
        far = 1 if side == 1 else 2
        pieces[far] = pieces[far] + decode(refs["in"][12], refs["in_steps"][4])
        return pieces

    def z_second(refs, pieces, rows):
        code, refs["steps"][1] = encode(jnp.concatenate(pieces[1:], axis=0))
        refs["codes2"][...] = code.reshape(2, rows, 128).astype(jnp.int16)
        refs["own"][...] = pieces[0]
        started = []
        for n, o in enumerate((5, -5)):
            started.append(link(refs["steps"].at[1], refs["in_steps"].at[5 + n], z_at(o)))
            started.append(link(refs["codes2"].at[n], refs["in2"].at[n], z_at(o)))
        begin(started)
        return started

    def z_end(refs, started):
        arrive(started)
        value = refs["own"][...]
        for n in range(2):
            value = value + decode(refs["in2"][n], refs["in_steps"][5 + n])
        return value

    refs_b = parts[-1]
    zb = refs_b["z"]
    rb = (share - sum(RUNS)) * lanes
    sums_b = refs_b["sums"]

    def b_at(d):
        return sums_b[pl.ds(pl.multiple_of(d * NX * rb, 8), NX * rb), :]

    one, two = AlongX(0), AlongX(1)
    one.opposite()
    gradient(sums_b, starts[-1], NX * nz * (rb // lanes))
    started_b = z_start(zb, sums_b[...], NX * rb, -1)
    one.near()
    two.opposite()
    one.relay()
    two.near()
    one.gradient(x)
    two.gradient(x)
    two.relay()
    one.finish()
    started_1 = z_start(one.z, one.sums[x], one.chunk, 1)
    two.finish()
    started_2 = z_start(two.z, two.sums[x], two.chunk, 1)

    pieces = z_middle(zb, started_b, b_at, -1)
    value = jnp.concatenate([p.reshape(NX, rb, 128) for p in pieces], axis=1)
    refs_b["x_own"][...] = value
    code, refs_b["x_steps"][0] = encode(value.reshape(NX * 3 * rb, 128))
    refs_b["x_codes"][...] = code.reshape(NX, 3 * rb, 128).astype(jnp.int16)
    across = []
    for n, dx in enumerate((2, 1, 3)):
        across.append(link(refs_b["x_steps"].at[0], refs_b["x_steps"].at[1 + n], x_at(dx)))
        across.append(link(refs_b["x_codes"].at[(x + dx) % NX], refs_b["x_in"].at[n], x_at(dx)))
    begin(across)

    pieces = z_middle(one.z, started_1, one.at, 1)
    started_1 = z_second(one.z, pieces, one.chunk)
    pieces = z_middle(two.z, started_2, two.at, 1)
    started_2 = z_second(two.z, pieces, two.chunk)
    arrive(across)
    value = refs_b["x_own"][x]
    for n in range(3):
        value = value + decode(refs_b["x_in"][n], refs_b["x_steps"][1 + n])
    started_b = z_second(zb, [value[n * rb : (n + 1) * rb, :] for n in range(3)], rb)
    out_ref[0 : one.chunk, :] = z_end(one.z, started_1)
    out_ref[one.chunk : one.chunk + two.chunk, :] = z_end(two.z, started_2)
    out_ref[one.chunk + two.chunk :, :] = z_end(zb, started_b)
    for copy in copies:
        copy.wait_send()


def shards(nz, grad_out, routes, route_weight, example_ids, example_weight, hidden):
    tok, dw = grad_out.shape
    cap, ff = hidden.shape[3:]
    lanes = dw // 128
    share = ff // (NX * nz)
    half = nz // 2
    i16 = jnp.int16

    def z_refs(rows, last):
        return dict(
            codes=pltpu.VMEM((nz, rows, 128), i16),
            steps=pltpu.VMEM((2, 1, 128), F32),
            **{"in": pltpu.VMEM((13, rows, 128), i16)},
            in_steps=pltpu.VMEM((7, 1, 128), F32),
            codes2=pltpu.VMEM((2, last, 128), i16),
            in2=pltpu.VMEM((2, last, 128), i16),
            own=pltpu.VMEM((last, 128), F32),
        )

    parts = []
    for rows in RUNS:
        chunk = rows * lanes
        parts.append(dict(
            sums=pltpu.VMEM((NX, nz * chunk, 128), F32),
            x_codes=pltpu.VMEM((6, half * chunk, 128), i16),
            x_steps=pltpu.VMEM((6, 1, 128), F32),
            x_in=pltpu.VMEM((6, half * chunk, 128), i16),
            x_in_steps=pltpu.VMEM((6, 1, 128), F32),
            z=z_refs(chunk, chunk),
        ))
    rb = (share - sum(RUNS)) * lanes
    parts.append(dict(
        sums=pltpu.VMEM((nz * NX * rb, 128), F32),
        x_own=pltpu.VMEM((NX, 3 * rb, 128), F32),
        x_codes=pltpu.VMEM((NX, 3 * rb, 128), i16),
        x_in=pltpu.VMEM((3, 3 * rb, 128), i16),
        x_steps=pltpu.VMEM((4, 1, 128), F32),
        z=z_refs(NX * rb, rb),
    ))
    dma = pltpu.SemaphoreType.DMA
    scratch = [
        pltpu.VMEM((tok, dw), BF16),
        pltpu.VMEM((TOP, tok), jnp.int32),
        pltpu.VMEM((TOP, tok), F32),
        pltpu.VMEM((1, tok), jnp.int32),
        pltpu.VMEM((1, EXAMPLES), F32),
        pltpu.VMEM((8, cap, ff), BF16),
        pltpu.VMEM((8, tok), F32),
        pltpu.VMEM((8, tok), F32),
        pltpu.VMEM((8, 128), F32),
        pltpu.VMEM((8, 128), F32),
        pltpu.VMEM((7, cap, dw), BF16),
        pltpu.VMEM((2, cap, dw), BF16),
        pltpu.VMEM((8, cap, dw), BF16),
        pltpu.VMEM((7, 2, 128), F32),
        pltpu.VMEM((8, 2, 128), F32),
        pltpu.VMEM((1, 128), F32),
        pltpu.VMEM((7, 1, 128), F32),
        pltpu.VMEM((8 * cap, 8 * cap), F32),
        pltpu.VMEM((ff, 8 * cap), BF16),
        pltpu.VMEM((8 * cap, dw), BF16),
        parts,
        dma((13,)), dma((LINKS,)), dma((LINKS,)),
    ]
    out = pl.pallas_call(
        functools.partial(body, (nz, ff, dw, cap, tok)),
        out_shape=jax.ShapeDtypeStruct((share * lanes, 128), F32),
        in_specs=[pl.BlockSpec(memory_space=pl.ANY)] * 6,
        out_specs=pl.BlockSpec(memory_space=pltpu.VMEM),
        scratch_shapes=scratch,
        compiler_params=pltpu.CompilerParams(
            collective_id=0, has_side_effects=True, vmem_limit_bytes=62 * 1024 * 1024
        ),
        name="clipped_grads",
    )(grad_out, routes.T, route_weight.T, example_ids, example_weight, hidden[0, 0])
    return out.reshape(share, 1, dw)


def solution(mesh):
    nz = mesh.shape["dp"] // NX
    placed = (
        P(("dp", "expert"), None),
        P(("dp", "expert"), None),
        P(("dp", "expert"), None),
        P("dp", "expert"),
        P("dp", None),
        P("dp", "expert", None, None, None),
    )
    return jax.shard_map(
        functools.partial(shards, nz), mesh=mesh, in_specs=placed,
        out_specs=P("dp", "expert", None), check_vma=False,
    )
```

time: 61.8 us -> 54.9 us (0.89)
  Pallas kernels: 59.9 us -> 53.1 us
    pallas_call x1, Pallas kernels: 59.9 us -> 53.1 us  [shards(): pl.pallas_call(functools.partial(body, (nz, ff, dw, cap, tok)), out_shape...]
where the time goes in v3:
time: 54.9 us; the launch traced here: 54.5 us
  Pallas kernels  53.1 us (97%)
  local copies, waits for them, and re-layouts  1.41 us (3%)
    pallas_call x1, Pallas kernels, shards(): pl.pallas_call(functools.partial(body, (nz, ff, dw, cap, tok)), out_shape...  53.1 us
    unnamed x1, local copies, waits for them, and re-layouts  1.41 us

profile of v3, /device:TPU:24, one launch (start us, length us, event | category | flops | bytes accessed | tf_op | source)
XLA Modules:
  0.0 54.5 jit_solution(4684207766760799075)
XLA Ops:
  0.0 53.1 %clipped_grads.1 = f32[88,128]{1,0:T(8,128)} custom-call(bf16[256,1024]{1,0:T(8,128)(2,1)} %go_hbm.1, s32[6,256]{1,0:T(8,128)} %bitcast.6, f32[6,256]{1,0:T(8,128)} %bitcast.7, s32[1,256]{1,0:T(1,128)} %ids_hbm.1, f32[1,8]{1,0:T(1,128)} %ew_hbm.1, bf16[8,48,704]{2,1,0:T(8,128)(2,1)} %bitcast.4), custom_call_target="tpu_custom_call" | custom-call | tf_op jit(solution)/shard_map/clipped_grads/pallas_call | solution.py:457
  53.1 1.4 %copy.10 = f32[11,1,1024]{2,1,0:T(1,128)} copy(f32[11,1,1024]{2,1,0:T(1,128)} %bitcast.5) | data formatting | bytes 90112

commit v4 on v3

--- a/solution.py
+++ b/solution.py
@@ -14,8 +14,9 @@
 F32 = jnp.float32
 BF16 = jnp.bfloat16
 
-RUNS = (4, 3)
-LINKS = 128
+RUNS = (4, 4)
+LINKS = 112
+STRIDE = 5
 
 REL = ((2, 0), (2, 1), (1, 0), (3, 0), (1, 1), (3, 1), (0, 1), (0, 0))
 
@@ -182,7 +183,12 @@
         r = at - rows * q
         if n == len(RUNS):
             zq = jnp.floor((q + 0.5) * (1.0 / NX))
-            q = nz * (q - NX * zq) + zq
+            xq = q - NX * zq
+        else:
+            xq = jnp.floor((q + 0.5) * (1.0 / nz))
+            zq = q - nz * xq
+        zq = STRIDE * zq
+        q = nz * xq + zq - nz * jnp.floor((zq + 0.5) * (1.0 / nz))
         unit = jnp.where(j >= start, share * q + taken + r, unit)
         starts.append(start)
         start, taken = start + NX * nz * rows, taken + rows
@@ -293,33 +299,37 @@
             self.sums[x, self.lower, :] = self.sums[x, self.lower, :] + (self.value(4) + self.value(3))
             self.sums[x, self.upper, :] = self.sums[x, self.upper, :] + (self.value(2) + self.value(5))
 
-        def at(self, d):
-            return self.sums[x, pl.ds(pl.multiple_of(d * self.chunk, 8), self.chunk), :]
+        def at(self, n):
+            return self.sums[x, pl.ds(pl.multiple_of(n * self.chunk, 8), self.chunk), :]
+
+    def place(d):
+        return (pow(STRIDE, -1, nz) * (z + nz + d)) % nz
 
     def z_start(refs, sums, rows, side):
         code, refs["steps"][0] = encode(sums)
-        refs["codes"][...] = code.reshape(nz, rows, 128).astype(jnp.int16)
-        plan = [(o, n, ((0, 0), (5, 1), (-5, 2))) for o, n in ((2, 0), (-2, 1), (1, 2), (-1, 3))]
-        plan.insert(2, (3 * side, 4, ((5 * side, 0),)))
+        code = code.reshape(nz, rows, 128).astype(jnp.int16)
+        refs["codes"][1 : nz + 1] = code
+        refs["codes"][0] = code[nz - 1]
+        refs["codes"][nz + 1] = code[0]
         started = []
-        for o, n, wanted in plan:
+        for n, o in enumerate((2, -2, 3 * side, 1, -1)):
             started.append(link(refs["steps"].at[0], refs["in_steps"].at[n], z_at(o)))
-            for d, m in wanted:
-                started.append(
-                    link(refs["codes"].at[(z + nz + o + d) % nz], refs["in"].at[3 * n + m], z_at(o))
-                )
+            if n == 2:
+                src, dst = refs["codes"].at[1 + place(half)], refs["in_far"]
+            else:
+                src, dst = refs["codes"].at[pl.ds(place(o), 3)], refs["in"].at[n - n // 3]
+            started.append(link(src, dst, z_at(o)))
         begin(started)
         return started
 
     def z_middle(refs, started, sums_at, side):
         arrive(started)
-        pieces = [sums_at(z), sums_at((z + 5) % nz), sums_at((z + nz - 5) % nz)]
+        pieces = [sums_at((place(0) + nz + d) % nz) for d in (-1, 0, 1)]
         for n in range(4):
             for m in range(3):
-                pieces[m] = pieces[m] + decode(refs["in"][3 * n + m], refs["in_steps"][n])
-        far = 1 if side == 1 else 2
-        pieces[far] = pieces[far] + decode(refs["in"][12], refs["in_steps"][4])
-        return pieces
+                pieces[m] = pieces[m] + decode(refs["in"][n, m], refs["in_steps"][n + n // 2])
+        pieces[1 + side] = pieces[1 + side] + decode(refs["in_far"][...], refs["in_steps"][2])
+        return pieces[1], pieces[2], pieces[0]
 
     def z_second(refs, pieces, rows):
         code, refs["steps"][1] = encode(jnp.concatenate(pieces[1:], axis=0))
@@ -344,8 +354,8 @@
     rb = (share - sum(RUNS)) * lanes
     sums_b = refs_b["sums"]
 
-    def b_at(d):
-        return sums_b[pl.ds(pl.multiple_of(d * NX * rb, 8), NX * rb), :]
+    def b_at(n):
+        return sums_b[pl.ds(pl.multiple_of(n * NX * rb, 8), NX * rb), :]
 
     one, two = AlongX(0), AlongX(1)
     one.opposite()
@@ -400,9 +410,10 @@
 
     def z_refs(rows, last):
         return dict(
-            codes=pltpu.VMEM((nz, rows, 128), i16),
+            codes=pltpu.VMEM((nz + 2, rows, 128), i16),
             steps=pltpu.VMEM((2, 1, 128), F32),
-            **{"in": pltpu.VMEM((13, rows, 128), i16)},
+            **{"in": pltpu.VMEM((4, 3, rows, 128), i16)},
+            in_far=pltpu.VMEM((rows, 128), i16),
             in_steps=pltpu.VMEM((7, 1, 128), F32),
             codes2=pltpu.VMEM((2, last, 128), i16),
             in2=pltpu.VMEM((2, last, 128), i16),

time: 54.9 us -> 53.7 us (0.978)
  Pallas kernels: 53.1 us -> 51.8 us
    pallas_call x1, Pallas kernels: 53.1 us -> 51.8 us  [shards(): pl.pallas_call(functools.partial(body, (nz, ff, dw, cap, tok)), out_shape...]
where the time goes in v4:
time: 53.7 us; the launch traced here: 53.2 us
  Pallas kernels  51.8 us (96%)
  local copies, waits for them, and re-layouts  1.41 us (3%)
    pallas_call x1, Pallas kernels, shards(): pl.pallas_call(functools.partial(body, (nz, ff, dw, cap, tok)), out_shape...  51.8 us
    unnamed x1, local copies, waits for them, and re-layouts  1.41 us

profile of v4, /device:TPU:24, one launch (start us, length us, event | category | flops | bytes accessed | tf_op | source)
XLA Modules:
  0.0 53.2 jit_solution(5436464346225272972)
XLA Ops:
  0.0 51.8 %clipped_grads.1 = f32[88,128]{1,0:T(8,128)} custom-call(bf16[256,1024]{1,0:T(8,128)(2,1)} %go_hbm.1, s32[6,256]{1,0:T(8,128)} %bitcast.6, f32[6,256]{1,0:T(8,128)} %bitcast.7, s32[1,256]{1,0:T(1,128)} %ids_hbm.1, f32[1,8]{1,0:T(1,128)} %ew_hbm.1, bf16[8,48,704]{2,1,0:T(8,128)(2,1)} %bitcast.4), custom_call_target="tpu_custom_call" | custom-call | tf_op jit(solution)/shard_map/clipped_grads/pallas_call | solution.py:468
  51.8 1.4 %copy.10 = f32[11,1,1024]{2,1,0:T(1,128)} copy(f32[11,1,1024]{2,1,0:T(1,128)} %bitcast.5) | data formatting | bytes 90112

commit v5 on v4

--- a/solution.py
+++ b/solution.py
@@ -57,7 +57,7 @@
     out_ref,
     go_ref, routes_ref, weight_ref, ids_ref, ew_ref,
     h_buf, rank_s, scale_s, lo_s, hi_s, send_buf, relay_buf, c_buf, meta_send, meta_recv, sq_send, sq_recv,
-    gl_s, ht_s, scaled_s, parts,
+    gl_head, gl_rest, ht_s, scaled_s, parts,
     local_sem, send_sem, recv_sem,
 ):
     nz, ff, dw, cap, tok = cfg
@@ -84,12 +84,6 @@
         n = len(copies)
         copies.append(other(src, dst, send_sem.at[n], recv_sem.at[n], **place))
         return copies[-1]
-
-    barrier = pltpu.get_barrier_semaphore()
-    greeted = [expert_at(dy, dc) for dy, dc in REL[:7]]
-    greeted += [x_at(dx) for dx in (1, 2, 3)] + [z_at(dz) for dz in (1, -1, 2, -2, 3, -3)]
-    for place in greeted:
-        pl.semaphore_signal(barrier, inc=1, device_id=place, device_id_type=MESH)
 
     inputs = [
         pltpu.make_async_copy(src, dst, local_sem.at[n])
@@ -100,6 +94,12 @@
     ]
     for copy in inputs:
         copy.start()
+    barrier = pltpu.get_barrier_semaphore()
+    greeted = [expert_at(dy, dc) for dy, dc in REL[:7]]
+    greeted += [x_at(dx) for dx in (1, 2, 3)] + [z_at(dz) for dz in (1, -1, 2, -2, 3, -3)]
+    for place in greeted:
+        pl.semaphore_signal(barrier, inc=1, device_id=place, device_id_type=MESH)
+
     h_copies = [
         pltpu.make_async_copy(h_ref.at[source[p]], h_buf.at[p], local_sem.at[5 + p])
         for p in range(8)
@@ -172,7 +172,10 @@
     for copy in h_copies:
         copy.wait()
     h = h_buf[...].reshape(8 * cap, ff)
-    gl_s[...] = nt_dot(h, h)
+    late = 2 * cap
+    head, rest = h[:late], h[late:]
+    gl_head[...] = nt_dot(head, h)
+    gl_rest[...] = nt_dot(rest, rest)
     share = ff // (NX * nz)
     j = iota((ff, 1), 0).astype(F32)
     unit, start, taken = j, 0, 0
@@ -211,14 +214,19 @@
         axis=0,
     )
     member_b = member.astype(BF16)
-    gl_s[...] = gl_s[...] * nt_dot(member_b, member_b)
+    twice = jnp.where(iota((late, 8 * cap), 1) < late, 1.0, 2.0)
+    gl_head[...] = gl_head[...] * (twice * nt_dot(member_b[:late], member_b))
+    gl_rest[...] = gl_rest[...] * nt_dot(member_b[late:], member_b[late:])
     for p in range(2, 7):
         c_copies[p].wait_recv()
+    rest = c_buf[2:8].reshape(6 * cap, dw)
+    spread = jnp.sum(gl_rest[...] * nt_dot(rest, rest), axis=1, keepdims=True)
+    squares = jnp.sum(member[late:] * spread, axis=0, keepdims=True)
     for copy in relays:
         copy.wait_recv()
     cot = c_buf[...].reshape(8 * cap, dw)
-    spread = jnp.sum(gl_s[...] * nt_dot(cot, cot), axis=1, keepdims=True)
-    squares = jnp.sum(member * spread, axis=0, keepdims=True)
+    spread = jnp.sum(gl_head[...] * nt_dot(cot[:late], cot), axis=1, keepdims=True)
+    squares = squares + jnp.sum(member[:late] * spread, axis=0, keepdims=True)
     sq_send[...] = squares
     q_copies = [link(sq_send, sq_recv.at[p], expert_at(*REL[p])) for p in range(7)]
     for copy in q_copies:
@@ -393,10 +401,13 @@
     for n in range(3):
         value = value + decode(refs_b["x_in"][n], refs_b["x_steps"][1 + n])
     started_b = z_second(zb, [value[n * rb : (n + 1) * rb, :] for n in range(3)], rb)
+    sent = len(copies) - 12
+    for copy in copies[:sent]:
+        copy.wait_send()
     out_ref[0 : one.chunk, :] = z_end(one.z, started_1)
     out_ref[one.chunk : one.chunk + two.chunk, :] = z_end(two.z, started_2)
     out_ref[one.chunk + two.chunk :, :] = z_end(zb, started_b)
-    for copy in copies:
+    for copy in copies[sent:]:
         copy.wait_send()
 
 
@@ -459,7 +470,8 @@
         pltpu.VMEM((8, 2, 128), F32),
         pltpu.VMEM((1, 128), F32),
         pltpu.VMEM((7, 1, 128), F32),
-        pltpu.VMEM((8 * cap, 8 * cap), F32),
+        pltpu.VMEM((2 * cap, 8 * cap), F32),
+        pltpu.VMEM((6 * cap, 6 * cap), F32),
         pltpu.VMEM((ff, 8 * cap), BF16),
         pltpu.VMEM((8 * cap, dw), BF16),
         parts,

time: 53.7 us -> 53.4 us (level)
  no operation moved by 1% of the time
where the time goes in v5:
time: 53.4 us; the launch traced here: 53 us
  Pallas kernels  51.6 us (97%)
  local copies, waits for them, and re-layouts  1.41 us (3%)
    pallas_call x1, Pallas kernels, shards(): pl.pallas_call(functools.partial(body, (nz, ff, dw, cap, tok)), out_shape...  51.6 us
    unnamed x1, local copies, waits for them, and re-layouts  1.41 us

profile of v5, /device:TPU:24, one launch (start us, length us, event | category | flops | bytes accessed | tf_op | source)
XLA Modules:
  0.0 53.0 jit_solution(11233101228237579064)
XLA Ops:
  0.0 51.6 %clipped_grads.1 = f32[88,128]{1,0:T(8,128)} custom-call(bf16[256,1024]{1,0:T(8,128)(2,1)} %go_hbm.1, s32[6,256]{1,0:T(8,128)} %bitcast.6, f32[6,256]{1,0:T(8,128)} %bitcast.7, s32[1,256]{1,0:T(1,128)} %ids_hbm.1, f32[1,8]{1,0:T(1,128)} %ew_hbm.1, bf16[8,48,704]{2,1,0:T(8,128)(2,1)} %bitcast.4), custom_call_target="tpu_custom_call" | custom-call | tf_op jit(solution)/shard_map/clipped_grads/pallas_call | solution.py:480
  51.6 1.4 %copy.10 = f32[11,1,1024]{2,1,0:T(1,128)} copy(f32[11,1,1024]{2,1,0:T(1,128)} %bitcast.5) | data formatting | bytes 90112
